TPU v7x, 32 devices: a whole 2x2x4 slice. The times are simulated.
32 devices in a mesh: groups: 2 (over y), dp: 4 (over x, core), mp: 4 (over z).
Axes of the slice: x: 2, y: 2, z: 4, core: 2. Of those that a mesh axis runs over, the one named last changes fastest.
Arguments:
- base_states: bfloat16 [1280, 4096], P(('groups', 'dp'), 'mp'), parts along dimension 0, may hold values from -6 to 6
- source_states: bfloat16 [1280, 4096], P(('groups', 'dp'), 'mp'), parts along dimension 0, may hold values from -6 to 6
- source_rank: int32 [1280, 1], P(('groups', 'dp')), parts along dimension 0, may hold values from 0 to 3; in each aligned block of 160 rows (0 to 159, 160 to 319, ...) at most 80 rows name the same one
- source_row: int32 [1280], P(('groups', 'dp')), parts along dimension 0, may hold values from 0 to 159
- rotation: bfloat16 [4096, 4096], P(None, 'mp'), may hold values from -0.125 to 0.125
- mask_logits: float32 [4096], P('mp'), may hold values from -8 to 8
- norm_gain: bfloat16 [4096], replicated, may hold values from 0.25 to 1.75
- gate_weight: bfloat16 [4096, 14336], P(None, 'mp'), may hold values from -0.09375 to 0.09375
- up_weight: bfloat16 [4096, 14336], P(None, 'mp'), may hold values from -0.09375 to 0.09375
- hidden_cot: bfloat16 [1280, 14336], P(('groups', 'dp'), 'mp'), parts along dimension 0, may hold values from -0.23632812 to 0.23632812
Outputs:
- rotation_grad: float32 [8192, 4096], P(('groups', 'dp'), 'mp'), parts along dimension 0
- interchanged: bfloat16 [1280, 4096], P(('groups', 'dp'), 'mp'), parts along dimension 0
There are 2 independent parts, one for each index of `groups`. A program takes and returns all parts, laid end to end along the dimension named above; an argument that names none is the same for every part. Nothing has to cross between parts.
Inputs may be any that keep to these rules, and one draw needn't show every extreme that they name: `source_rank`: within the 160 tokens of each dp index, no dp index is named more than 80 times, and some dp index is named exactly 80 times by the tokens of some dp index.
All inputs are finite; a program needn't handle non-finite values.
Results may differ from a plain program's by a relative error of at most 0.014.
Values may be sent and summed in bfloat16 or wider, within the bound.
A program may use at most 192 MiB of HBM per device.

v0:
```python
import jax
import jax.numpy as jnp
from jax import lax
from jax.sharding import PartitionSpec as P


def contract_first(left, right):
    return lax.dot_general(
        left, right, (((0,), (0,)), ((), ())), preferred_element_type=jnp.float32
    )


def contract_last(left, right):
    return lax.dot_general(
        left, right, (((1,), (1,)), ((), ())), preferred_element_type=jnp.float32
    )


def shards(
    base_states,
    source_states,
    source_rank,
    source_row,
    rotation,
    mask_logits,
    norm_gain,
    gate_weight,
    up_weight,
    hidden_cot,
):
    tokens = base_states.shape[0]
    width = rotation.shape[0]
    ranks_of = source_rank[:, 0]
    everyone = lax.all_gather(source_states, "dp", axis=0, tiled=True)
    paired = jnp.take(everyone, ranks_of * tokens + source_row, axis=0)
    diff_local = (paired.astype(jnp.float32) - base_states.astype(jnp.float32)).astype(jnp.bfloat16)
    diff_full = lax.all_gather(diff_local, "mp", axis=1, tiled=True)
    mask = jax.nn.sigmoid(mask_logits)[None, :]
    coords = jnp.dot(diff_full, rotation, preferred_element_type=jnp.float32)
    weighted = (mask * coords).astype(jnp.bfloat16)
    moved = lax.psum_scatter(
        contract_last(rotation, weighted), "mp", scatter_dimension=0, tiled=True
    ).T
    interchanged = (base_states.astype(jnp.float32) + moved).astype(jnp.bfloat16)
    full_rows = lax.all_gather(interchanged, "mp", axis=1, tiled=True)
    states = full_rows.astype(jnp.float32)
    gain_f = norm_gain.astype(jnp.float32)[None, :]
    recip = lax.rsqrt(jnp.mean(states * states, axis=1, keepdims=True) + 1e-05)
    normed = (states * recip * gain_f).astype(jnp.bfloat16)
    gate = jnp.dot(normed, gate_weight, preferred_element_type=jnp.float32)
    up_val = jnp.dot(normed, up_weight, preferred_element_type=jnp.float32)
    sigm = jax.nn.sigmoid(gate)
    cotan = hidden_cot.astype(jnp.float32)
    dgate = (cotan * up_val * sigm * (1.0 + gate * (1.0 - sigm))).astype(jnp.bfloat16)
    dup_val = (cotan * gate * sigm).astype(jnp.bfloat16)
    partial_grad = contract_last(dgate, gate_weight) + contract_last(dup_val, up_weight)
    dnormed = lax.psum(partial_grad, "mp")
    scaled = gain_f * dnormed
    stat = jnp.sum(scaled * states, axis=1, keepdims=True)
    dinter = (recip * scaled - states * recip * recip * recip * stat / width).astype(jnp.bfloat16)
    coupled = (mask * jnp.dot(dinter, rotation, preferred_element_type=jnp.float32)).astype(
        jnp.bfloat16
    )
    rotation_grad = lax.psum_scatter(
        (contract_first(dinter, weighted) + contract_first(diff_full, coupled)).astype(
            jnp.bfloat16
        ),
        "dp",
        scatter_dimension=0,
        tiled=True,
    ).astype(jnp.float32)
    return (rotation_grad, interchanged)


def solution(mesh):
    placed = (
        P(("groups", "dp"), "mp"),
        P(("groups", "dp"), "mp"),
        P(("groups", "dp"), None),
        P(("groups", "dp")),
        P(None, "mp"),
        P("mp"),
        P(),
        P(None, "mp"),
        P(None, "mp"),
        P(("groups", "dp"), "mp"),
    )
    return jax.shard_map(
        shards,
        mesh=mesh,
        in_specs=placed,
        out_specs=(P(("groups", "dp"), "mp"), P(("groups", "dp"), "mp")),
        check_vma=False,
    )
```

profile of v0, /device:TPU:0, one launch (start us, length us, event | category | flops | bytes accessed | tf_op | source)
XLA Modules:
  0.0 437.6 jit_solution(6503187175433024214)
XLA Ops:
  7.2 0.0 all-gather.4.cloned.1.call-start
  7.2 0.7 all-gather.4.cloned.1.call-update
  7.9 0.0 all-gather.6.cloned.1.call-start
  8.0 0.7 broadcast_multiply_fusion
  8.6 0.7 compare_and_fusion
  9.3 21.2 %all-gather.4.cloned.1.call-done = bf16[640,1024]{1,0:T(8,128)(2,1)} async-done(((bf16[160,1024]{1,0:T(8,128)(2,1)}), bf16[640,1024]{1,0:T(8,128)(2,1)}) %all-gather.4.cloned.1.call-update) | async-done | bytes 1310736 | tf_op jit(solution)/shard_map/all_gather | solution.py:34
  30.5 2.7 gather_fusion
  33.2 0.9 fusion.25
  34.1 0.0 all-gather.6.cloned.1.call-update
  34.1 0.0 reduce-scatter.3.cloned.1.call-start
  34.2 32.8 %all-gather.6.cloned.1.call-done = bf16[160,4096]{1,0:T(8,128)(2,1)} async-done(((bf16[160,1024]{1,0:T(8,128)(2,1)}), bf16[160,4096]{1,0:T(8,128)(2,1)}) %all-gather.6.cloned.1.call-update) | async-done | bytes 1310736 | tf_op jit(solution)/shard_map/all_gather | solution.py:37
  66.9 5.3 %fusion.20 = bf16[160,1024]{1,0:T(8,128)(2,1)S(1)} fusion(bf16[160,4096]{1,0:T(8,128)(2,1)} %all-gather.6.cloned.1.call-done, bf16[4096,1024]{1,0:T(8,128)(2,1)} %param.14, f32[1024]{0:T(1024)S(1)} %add_divide_fusion.2), kind=kOutput, calls=%fused_computation.32 | convolution fusion | flops 1342504960 | bytes 10031104 | tf_op jit(solution)/shard_map/dot_general | solution.py:39
  72.3 7.8 %convolution_bitcast_fusion = f32[4096,160]{0,1:T(8,128)} fusion(bf16[160,1024]{1,0:T(8,128)(2,1)S(1)} %fusion.20, bf16[4096,1024]{1,0:T(8,128)(2,1)} %param.14), kind=kOutput, calls=%fused_computation.5 | convolution fusion | flops 1342177280 | bytes 11337728 | tf_op jit(solution)/shard_map/dot_general | solution.py:14
  80.1 0.0 reduce-scatter.3.cloned.1.call-update
  80.1 0.0 all-gather.8.cloned.1.call-start
  80.1 51.2 %reduce-scatter.3.cloned.1.call-done = f32[1024,160]{0,1:T(8,128)} async-done(((f32[4096,160]{0,1:T(8,128)}), f32[1024,160]{0,1:T(8,128)}) %reduce-scatter.3.cloned.1.call-update) | async-done | bytes 655376 | tf_op jit(solution)/shard_map/reduce_scatter | solution.py:41
  131.3 1.9 fusion.26
  133.3 0.2 all-reduce.2.cloned.1.call-start
  133.5 32.3 %all-gather.8.cloned.1.call-done = bf16[160,4096]{1,0:T(8,128)(2,1)} async-done(((bf16[160,1024]{1,0:T(8,128)(2,1)}), bf16[160,4096]{1,0:T(8,128)(2,1)}) %all-gather.8.cloned.1.call-update) | async-done | bytes 1310736 | tf_op jit(solution)/shard_map/all_gather | solution.py:45
  165.8 1.7 fusion.13
  167.5 16.2 %fusion.27 = f32[160,3584]{1,0:T(8,128)} fusion(bf16[4096,3584]{1,0:T(8,128)(2,1)} %param.17, bf16[160,4096]{1,0:T(8,128)(2,1)} %all-gather.8.cloned.1.call-done, f32[4096]{0:T(1024)S(1)} %convert_element_type.52, f32[160]{0:T(256)S(1)} %add_rsqrt_fusion), kind=kOutput, calls=%fused_computation.40 | convolution fusion | flops 4700241920 | bytes 32981632 | tf_op jit(solution)/shard_map/dot_general | solution.py:50
  183.7 25.1 %fusion.3 = f32[160,4096]{1,0:T(8,128)} fusion(bf16[4096,3584]{1,0:T(8,128)(2,1)} %param.17, bf16[4096,3584]{1,0:T(8,128)(2,1)} %param.18, bf16[160,3584]{1,0:T(8,128)(2,1)S(1)} %copy-done.6, f32[160,3584]{1,0:T(8,128)} %fusion.27, bf16[160,4096]{1,0:T(8,128)(2,1)S(1)} %copy-done, f32[4096]{0:T(1024)S(1)} %convert_element_type.52, f32[160]{0:T(256)S(1)} %add_rsqrt_fusion), kind=kOutput, calls=%fused_computation.11 | convolution fusion | flops 9404170240 | bytes 66110080 | tf_op jit(solution)/shard_map/dot_general | solution.py:14
  208.8 16.1 %convolution_add_fusion = f32[160,4096]{1,0:T(8,128)} fusion(f32[160,4096]{1,0:T(8,128)} %fusion.3, bf16[4096,3584]{1,0:T(8,128)(2,1)} %param.18, f32[160,3584]{1,0:T(8,128)} %fusion.27, bf16[160,3584]{1,0:T(8,128)(2,1)S(1)} %copy-done.6), kind=kOutput, calls=%fused_computation.6 | convolution fusion | flops 4702289920 | bytes 38043648 | tf_op jit(solution)/shard_map/dot_general | solution.py:14
  224.9 0.3 reduce-scatter.5.cloned.1.call-start
  225.2 103.0 %all-reduce.2.cloned.1.call-done = f32[160,4096]{1,0:T(8,128)} async-done(((f32[160,4096]{1,0:T(8,128)}), f32[160,4096]{1,0:T(8,128)}) %all-reduce.2.cloned.1.call-update) | async-done | bytes 2621456 | tf_op jit(solution)/shard_map/psum | solution.py:57
  328.2 2.3 fusion.14
  330.5 0.2 copy-done.1
  330.7 5.3 %fusion.21 = bf16[160,1024]{1,0:T(8,128)(2,1)S(1)} fusion(bf16[4096,1024]{1,0:T(8,128)(2,1)} %param.14, f32[1024]{0:T(1024)S(1)} %add_divide_fusion.2, bf16[160,4096]{1,0:T(8,128)(2,1)S(1)} %copy-done, f32[160,4096]{1,0:T(8,128)S(1)} %copy-done.1, f32[160]{0:T(256)S(1)} %fusion.14, f32[4096]{0:T(1024)S(1)} %convert_element_type.52, f32[160]{0:T(256)S(1)} %add_rsqrt_fusion), kind=kOutput, calls=%fused_computation.33 | convolution fusion | flops 1349058560 | bytes 12670208 | tf_op jit(solution)/shard_map/dot_general | solution.py:61
  336.1 8.3 %fusion.34 = f32[4096,1024]{1,0:T(8,128)} fusion(bf16[160,1024]{1,0:T(8,128)(2,1)S(1)} %fusion.20, bf16[160,4096]{1,0:T(8,128)(2,1)S(1)} %copy-done, f32[160,4096]{1,0:T(8,128)S(1)} %copy-done.1, f32[160]{0:T(256)S(1)} %fusion.14, f32[4096]{0:T(1024)S(1)} %convert_element_type.52, f32[160]{0:T(256)S(1)} %add_rsqrt_fusion), kind=kOutput, calls=%fused_computation.49 | convolution fusion | flops 1348730880 | bytes 21054720 | tf_op jit(solution)/shard_map/dot_general | solution.py:8
  344.4 11.4 %add_convert_fusion = bf16[4096,1024]{1,0:T(8,128)(2,1)} fusion(f32[4096,1024]{1,0:T(8,128)} %fusion.34, bf16[160,4096]{1,0:T(8,128)(2,1)S(1)} %copy-done.2, bf16[160,1024]{1,0:T(8,128)(2,1)S(1)} %fusion.21), kind=kOutput, calls=%fused_computation.1 | convolution fusion | flops 1350565888 | bytes 26804224 | tf_op jit(solution)/shard_map/dot_general | solution.py:8
  355.8 70.9 %reduce-scatter.5.cloned.1.call-done = bf16[1024,1024]{1,0:T(8,128)(2,1)} async-done(((bf16[4096,1024]{1,0:T(8,128)(2,1)}), bf16[1024,1024]{1,0:T(8,128)(2,1)}) %reduce-scatter.5.cloned.1.call-update) | async-done | bytes 2097168 | tf_op jit(solution)/shard_map/reduce_scatter | solution.py:64
  426.7 4.1 convert_element_type.60
  (20 shorter events, 0.1 us)
Async XLA Ops:
  7.2 26.0 %copy-start.3 = (bf16[160,1024]{1,0:T(8,128)(2,1)S(1)}, bf16[160,1024]{1,0:T(8,128)(2,1)}, u32[]{:S(2)}) copy-start(bf16[160,1024]{1,0:T(8,128)(2,1)} %param.10) | copy-start | bytes 983044
  7.2 27.0 %copy-start.5 = (f32[1024]{0:T(1024)S(1)}, f32[1024]{0:T(1024)}, u32[]{:S(2)}) copy-start(f32[1024]{0:T(1024)} %param.15) | copy-start | bytes 12292
  7.2 23.3 %all-gather.4.cloned.1.call-start = ((), (), s32[]{:S(2)}) async-start(), calls=%async_computation.2 | async-start | bytes 1638400 | tf_op jit(solution)/shard_map/all_gather | solution.py:34
  7.9 59.0 %all-gather.6.cloned.1.call-start = ((), (), s32[]{:S(2)}) async-start(), calls=%async_computation.3 | async-start | bytes 1638400 | tf_op jit(solution)/shard_map/all_gather | solution.py:37
  34.1 97.3 %reduce-scatter.3.cloned.1.call-start = ((), (), s32[]{:S(2)}) async-start(), calls=%async_computation.4 | async-start | bytes 3276800 | tf_op jit(solution)/shard_map/reduce_scatter | solution.py:41
  80.1 53.4 %copy-start.4 = (bf16[4096]{0:T(1024)(128)(2,1)S(1)}, bf16[4096]{0:T(1024)(128)(2,1)}, u32[]{:S(2)}) copy-start(bf16[4096]{0:T(1024)(128)(2,1)} %param.16) | copy-start | bytes 24580
  80.1 85.7 %all-gather.8.cloned.1.call-start = ((), (), s32[]{:S(2)}) async-start(), calls=%async_computation.5 | async-start | bytes 1638400 | tf_op jit(solution)/shard_map/all_gather | solution.py:45
  133.3 194.9 %all-reduce.2.cloned.1.call-start = ((), (), s32[]{:S(2)}) async-start(), calls=%async_computation.6 | async-start | bytes 5242880 | tf_op jit(solution)/shard_map/psum | solution.py:57
  167.5 16.2 %copy-start = (bf16[160,4096]{1,0:T(8,128)(2,1)S(1)}, bf16[160,4096]{1,0:T(8,128)(2,1)}, u32[]{:S(2)}) copy-start(bf16[160,4096]{1,0:T(8,128)(2,1)} %all-gather.8.cloned.1.call-done) | copy-start | bytes 3932164
  167.5 16.2 %copy-start.6 = (bf16[160,3584]{1,0:T(8,128)(2,1)S(1)}, bf16[160,3584]{1,0:T(8,128)(2,1)}, u32[]{:S(2)}) copy-start(bf16[160,3584]{1,0:T(8,128)(2,1)} %param.19) | copy-start | bytes 3440644
  224.9 201.8 %reduce-scatter.5.cloned.1.call-start = ((), (), s32[]{:S(2)}) async-start(), calls=%async_computation.7 | async-start | bytes 10485760 | tf_op jit(solution)/shard_map/reduce_scatter | solution.py:64
  328.2 2.5 copy-start.1
  336.0 8.4 %copy-start.2 = (bf16[160,4096]{1,0:T(8,128)(2,1)S(1)}, bf16[160,4096]{1,0:T(8,128)(2,1)}, u32[]{:S(2)}) copy-start(bf16[160,4096]{1,0:T(8,128)(2,1)} %all-gather.6.cloned.1.call-done) | copy-start | bytes 3932164
Sparse Core Ops, SparseCore 0:
  9.6 20.8 all-gather.3
  34.2 32.6 all-gather.5
  80.2 51.0 reduce-scatter.2
  133.4 32.3 all-gather.7
  225.0 103.0 all-reduce.1
  355.9 70.7 reduce-scatter.4
where the time goes:
time: 438 us
  waiting for transfers between devices  312 us (71%)
  matrix products  95.6 us (22%)
  between operations  14.2 us (3%)
  other arithmetic  12.2 us (3%)
    psum x1, waiting for transfers between devices, shards(): dnormed = lax.psum(partial_grad, 'mp')  103 us
    reduce_scatter x1, waiting for transfers between devices, shards(): lax.psum_scatter((contract_first(dinter, weighted) + contract_first(diff_...  70.9 us
    reduce_scatter x1, waiting for transfers between devices, shards(): lax.psum_scatter(contract_last(rotation, weighted), 'mp', scatter_dimensi...  51.2 us
    dot_general x3, matrix products, contract_last(): lax.dot_general(left, right, (((1,), (1,)), ((), ())), preferred_element_...  49 us
    all_gather x1, waiting for transfers between devices, shards(): diff_full = lax.all_gather(diff_local, 'mp', axis=1, tiled=True)  32.8 us
    all_gather x1, waiting for transfers between devices, shards(): full_rows = lax.all_gather(interchanged, 'mp', axis=1, tiled=True)  32.3 us
    all_gather x1, waiting for transfers between devices, shards(): everyone = lax.all_gather(source_states, 'dp', axis=0, tiled=True)  21.2 us
    dot_general x2, matrix products, contract_first(): lax.dot_general(left, right, (((0,), (0,)), ((), ())), preferred_element_...  19.7 us
  transfers between devices with their start and end apart: 6, of which 6 were waited for; matrix products, arithmetic and copies ran while one was open for 0% of the time, Pallas kernels for 0%

commit v1 on v0

--- a/solution.py
+++ b/solution.py
@@ -2,6 +2,7 @@
 import jax.numpy as jnp
 from jax import lax
 from jax.sharding import PartitionSpec as P
+from jax.lax import all_gather
 
 
 def contract_first(left, right):
@@ -54,7 +55,7 @@
     dgate = (cotan * up_val * sigm * (1.0 + gate * (1.0 - sigm))).astype(jnp.bfloat16)
     dup_val = (cotan * gate * sigm).astype(jnp.bfloat16)
     partial_grad = contract_last(dgate, gate_weight) + contract_last(dup_val, up_weight)
-    dnormed = lax.psum(partial_grad, "mp")
+    dnormed = jnp.sum(all_gather(partial_grad, axis_name="mp"), axis=0)
     scaled = gain_f * dnormed
     stat = jnp.sum(scaled * states, axis=1, keepdims=True)
     dinter = (recip * scaled - states * recip * recip * recip * stat / width).astype(jnp.bfloat16)

time: 438 us -> 522 us (1.19)
  waiting for transfers between devices: 312 us -> 391 us
    all_gather x0 -> x1, waiting for transfers between devices: none -> 183 us  [shards(): dnormed = jnp.sum(all_gather(partial_grad, axis_name='mp'), axis=0)]
    psum x1 -> x0, waiting for transfers between devices: 103 us -> none  [shards(): dnormed = lax.psum(partial_grad, 'mp')]
where the time goes in v1:
time: 522 us; the launch traced here: 521 us
  waiting for transfers between devices  391 us (75%)
  matrix products  95.5 us (18%)
  other arithmetic  16.9 us (3%)
  between operations  14.2 us (3%)
    all_gather x1, waiting for transfers between devices, shards(): dnormed = jnp.sum(all_gather(partial_grad, axis_name='mp'), axis=0)  183 us
    reduce_scatter x1, waiting for transfers between devices, shards(): lax.psum_scatter((contract_first(dinter, weighted) + contract_first(diff_...  70.1 us
    reduce_scatter x1, waiting for transfers between devices, shards(): lax.psum_scatter(contract_last(rotation, weighted), 'mp', scatter_dimensi...  51.2 us
    dot_general x3, matrix products, contract_last(): lax.dot_general(left, right, (((1,), (1,)), ((), ())), preferred_element_...  48.9 us
    all_gather x1, waiting for transfers between devices, shards(): diff_full = lax.all_gather(diff_local, 'mp', axis=1, tiled=True)  32.8 us
    all_gather x1, waiting for transfers between devices, shards(): full_rows = lax.all_gather(interchanged, 'mp', axis=1, tiled=True)  32.3 us
    all_gather x1, waiting for transfers between devices, shards(): everyone = lax.all_gather(source_states, 'dp', axis=0, tiled=True)  21.2 us
    dot_general x2, matrix products, contract_first(): lax.dot_general(left, right, (((0,), (0,)), ((), ())), preferred_element_...  19.7 us
  transfers between devices with their start and end apart: 6, of which 6 were waited for; matrix products, arithmetic and copies ran while one was open for 0% of the time, Pallas kernels for 0%

profile of v1, /device:TPU:0, one launch (start us, length us, event | category | flops | bytes accessed | tf_op | source)
XLA Modules:
  0.0 521.0 jit_solution(2216762580217959727)
XLA Ops:
  7.2 0.0 all-gather.6.cloned.1.call-start
  7.2 0.7 all-gather.6.cloned.1.call-update
  7.9 0.0 all-gather.8.cloned.1.call-start
  8.0 0.7 broadcast_multiply_fusion
  8.6 0.7 compare_and_fusion
  9.3 21.2 %all-gather.6.cloned.1.call-done = bf16[640,1024]{1,0:T(8,128)(2,1)} async-done(((bf16[160,1024]{1,0:T(8,128)(2,1)}), bf16[640,1024]{1,0:T(8,128)(2,1)}) %all-gather.6.cloned.1.call-update) | async-done | bytes 1310736 | tf_op jit(solution)/shard_map/all_gather | solution.py:35
  30.5 2.7 gather_fusion
  33.2 0.9 fusion.25
  34.1 0.0 all-gather.8.cloned.1.call-update
  34.1 0.0 reduce-scatter.3.cloned.1.call-start
  34.2 32.8 %all-gather.8.cloned.1.call-done = bf16[160,4096]{1,0:T(8,128)(2,1)} async-done(((bf16[160,1024]{1,0:T(8,128)(2,1)}), bf16[160,4096]{1,0:T(8,128)(2,1)}) %all-gather.8.cloned.1.call-update) | async-done | bytes 1310736 | tf_op jit(solution)/shard_map/all_gather | solution.py:38
  66.9 5.3 %fusion.20 = bf16[160,1024]{1,0:T(8,128)(2,1)S(1)} fusion(bf16[160,4096]{1,0:T(8,128)(2,1)} %all-gather.8.cloned.1.call-done, bf16[4096,1024]{1,0:T(8,128)(2,1)} %param.14, f32[1024]{0:T(1024)S(1)} %add_divide_fusion.2), kind=kOutput, calls=%fused_computation.32 | convolution fusion | flops 1342504960 | bytes 10031104 | tf_op jit(solution)/shard_map/dot_general | solution.py:40
  72.3 7.8 %convolution_bitcast_fusion = f32[4096,160]{0,1:T(8,128)} fusion(bf16[160,1024]{1,0:T(8,128)(2,1)S(1)} %fusion.20, bf16[4096,1024]{1,0:T(8,128)(2,1)} %param.14), kind=kOutput, calls=%fused_computation.5 | convolution fusion | flops 1342177280 | bytes 11337728 | tf_op jit(solution)/shard_map/dot_general | solution.py:15
  80.1 0.0 reduce-scatter.3.cloned.1.call-update
  80.1 0.0 all-gather.10.cloned.1.call-start
  80.1 51.2 %reduce-scatter.3.cloned.1.call-done = f32[1024,160]{0,1:T(8,128)} async-done(((f32[4096,160]{0,1:T(8,128)}), f32[1024,160]{0,1:T(8,128)}) %reduce-scatter.3.cloned.1.call-update) | async-done | bytes 655376 | tf_op jit(solution)/shard_map/reduce_scatter | solution.py:42
  131.3 1.9 fusion.26
  133.3 0.2 all-gather.12.cloned.1.call-start
  133.5 32.3 %all-gather.10.cloned.1.call-done = bf16[160,4096]{1,0:T(8,128)(2,1)} async-done(((bf16[160,1024]{1,0:T(8,128)(2,1)}), bf16[160,4096]{1,0:T(8,128)(2,1)}) %all-gather.10.cloned.1.call-update) | async-done | bytes 1310736 | tf_op jit(solution)/shard_map/all_gather | solution.py:46
  165.8 1.7 fusion.13
  167.5 16.2 %fusion.27 = f32[160,3584]{1,0:T(8,128)} fusion(bf16[4096,3584]{1,0:T(8,128)(2,1)} %param.17, bf16[160,4096]{1,0:T(8,128)(2,1)} %all-gather.10.cloned.1.call-done, f32[4096]{0:T(1024)S(1)} %convert_element_type.52, f32[160]{0:T(256)S(1)} %add_rsqrt_fusion), kind=kOutput, calls=%fused_computation.40 | convolution fusion | flops 4700241920 | bytes 32981632 | tf_op jit(solution)/shard_map/dot_general | solution.py:51
  183.7 25.1 %fusion.3 = f32[160,4096]{1,0:T(8,128)} fusion(bf16[4096,3584]{1,0:T(8,128)(2,1)} %param.17, bf16[4096,3584]{1,0:T(8,128)(2,1)} %param.18, bf16[160,3584]{1,0:T(8,128)(2,1)S(1)} %copy-done.6, f32[160,3584]{1,0:T(8,128)} %fusion.27, bf16[160,4096]{1,0:T(8,128)(2,1)S(1)} %copy-done, f32[4096]{0:T(1024)S(1)} %convert_element_type.52, f32[160]{0:T(256)S(1)} %add_rsqrt_fusion), kind=kOutput, calls=%fused_computation.11 | convolution fusion | flops 9404170240 | bytes 66110080 | tf_op jit(solution)/shard_map/dot_general | solution.py:15
  208.8 16.1 %convolution_add_fusion = f32[160,4096]{1,0:T(8,128)} fusion(f32[160,4096]{1,0:T(8,128)} %fusion.3, bf16[4096,3584]{1,0:T(8,128)(2,1)} %param.18, f32[160,3584]{1,0:T(8,128)} %fusion.27, bf16[160,3584]{1,0:T(8,128)(2,1)S(1)} %copy-done.6), kind=kOutput, calls=%fused_computation.6 | convolution fusion | flops 4702289920 | bytes 38043648 | tf_op jit(solution)/shard_map/dot_general | solution.py:15
  224.9 0.3 reduce-scatter.5.cloned.1.call-start
  225.1 182.8 %all-gather.12.cloned.1.call-done = f32[640,4096]{1,0:T(8,128)} async-done(((f32[160,4096]{1,0:T(8,128)}), f32[640,4096]{1,0:T(8,128)}) %all-gather.12.cloned.1.call-update) | async-done | bytes 10485776 | tf_op jit(solution)/shard_map/all_gather | solution.py:58
  408.0 5.1 reduce_sum.28
  413.1 1.8 fusion.14
  414.9 5.3 %fusion.21 = bf16[160,1024]{1,0:T(8,128)(2,1)S(1)} fusion(bf16[4096,1024]{1,0:T(8,128)(2,1)} %param.14, f32[1024]{0:T(1024)S(1)} %add_divide_fusion.2, bf16[160,4096]{1,0:T(8,128)(2,1)S(1)} %copy-done.1, f32[160,4096]{1,0:T(8,128)S(1)} %reduce_sum.28, f32[160]{0:T(256)S(1)} %fusion.14, f32[4096]{0:T(1024)S(1)} %convert_element_type.52, ...), kind=kOutput, calls=%fused_computation.33 | convolution fusion | flops 1349058560 | bytes 12670208 | tf_op jit(solution)/shard_map/dot_general | solution.py:62
  420.3 8.3 %fusion.34 = f32[4096,1024]{1,0:T(8,128)} fusion(bf16[160,1024]{1,0:T(8,128)(2,1)S(1)} %fusion.20, bf16[160,4096]{1,0:T(8,128)(2,1)S(1)} %copy-done.1, f32[160,4096]{1,0:T(8,128)S(1)} %reduce_sum.28, f32[160]{0:T(256)S(1)} %fusion.14, f32[4096]{0:T(1024)S(1)} %convert_element_type.52, f32[160]{0:T(256)S(1)} %add_rsqrt_fusion), kind=kOutput, calls=%fused_computation.49 | convolution fusion | flops 1348730880 | bytes 21054720 | tf_op jit(solution)/shard_map/dot_general | solution.py:9
  428.6 11.4 %add_convert_fusion = bf16[4096,1024]{1,0:T(8,128)(2,1)} fusion(f32[4096,1024]{1,0:T(8,128)} %fusion.34, bf16[160,4096]{1,0:T(8,128)(2,1)S(1)} %copy-done.2, bf16[160,1024]{1,0:T(8,128)(2,1)S(1)} %fusion.21), kind=kOutput, calls=%fused_computation.1 | convolution fusion | flops 1350565888 | bytes 26804224 | tf_op jit(solution)/shard_map/dot_general | solution.py:9
  440.0 70.1 %reduce-scatter.5.cloned.1.call-done = bf16[1024,1024]{1,0:T(8,128)(2,1)} async-done(((bf16[4096,1024]{1,0:T(8,128)(2,1)}), bf16[1024,1024]{1,0:T(8,128)(2,1)}) %reduce-scatter.5.cloned.1.call-update) | async-done | bytes 2097168 | tf_op jit(solution)/shard_map/reduce_scatter | solution.py:65
  510.1 4.1 convert_element_type.60
  (21 shorter events, 0.1 us)
Async XLA Ops:
  7.2 26.0 %copy-start.3 = (bf16[160,1024]{1,0:T(8,128)(2,1)S(1)}, bf16[160,1024]{1,0:T(8,128)(2,1)}, u32[]{:S(2)}) copy-start(bf16[160,1024]{1,0:T(8,128)(2,1)} %param.10) | copy-start | bytes 983044
  7.2 27.0 %copy-start.5 = (f32[1024]{0:T(1024)S(1)}, f32[1024]{0:T(1024)}, u32[]{:S(2)}) copy-start(f32[1024]{0:T(1024)} %param.15) | copy-start | bytes 12292
  7.2 23.3 %all-gather.6.cloned.1.call-start = ((), (), s32[]{:S(2)}) async-start(), calls=%async_computation.2 | async-start | bytes 1638400 | tf_op jit(solution)/shard_map/all_gather | solution.py:35
  7.9 59.0 %all-gather.8.cloned.1.call-start = ((), (), s32[]{:S(2)}) async-start(), calls=%async_computation.3 | async-start | bytes 1638400 | tf_op jit(solution)/shard_map/all_gather | solution.py:38
  34.1 97.3 %reduce-scatter.3.cloned.1.call-start = ((), (), s32[]{:S(2)}) async-start(), calls=%async_computation.4 | async-start | bytes 3276800 | tf_op jit(solution)/shard_map/reduce_scatter | solution.py:42
  80.1 53.4 %copy-start.4 = (bf16[4096]{0:T(1024)(128)(2,1)S(1)}, bf16[4096]{0:T(1024)(128)(2,1)}, u32[]{:S(2)}) copy-start(bf16[4096]{0:T(1024)(128)(2,1)} %param.16) | copy-start | bytes 24580
  80.1 85.7 %all-gather.10.cloned.1.call-start = ((), (), s32[]{:S(2)}) async-start(), calls=%async_computation.5 | async-start | bytes 1638400 | tf_op jit(solution)/shard_map/all_gather | solution.py:46
  133.3 274.7 %all-gather.12.cloned.1.call-start = ((), (), s32[]{:S(2)}) async-start(), calls=%async_computation.7 | async-start | bytes 13107200 | tf_op jit(solution)/shard_map/all_gather | solution.py:58
  167.5 16.2 %copy-start = (bf16[160,4096]{1,0:T(8,128)(2,1)S(1)}, bf16[160,4096]{1,0:T(8,128)(2,1)}, u32[]{:S(2)}) copy-start(bf16[160,4096]{1,0:T(8,128)(2,1)} %all-gather.10.cloned.1.call-done) | copy-start | bytes 3932164
  167.5 16.2 %copy-start.6 = (bf16[160,3584]{1,0:T(8,128)(2,1)S(1)}, bf16[160,3584]{1,0:T(8,128)(2,1)}, u32[]{:S(2)}) copy-start(bf16[160,3584]{1,0:T(8,128)(2,1)} %param.19) | copy-start | bytes 3440644
  224.9 285.2 %reduce-scatter.5.cloned.1.call-start = ((), (), s32[]{:S(2)}) async-start(), calls=%async_computation.6 | async-start | bytes 10485760 | tf_op jit(solution)/shard_map/reduce_scatter | solution.py:65
  413.1 1.9 copy-start.1
  420.3 8.3 %copy-start.2 = (bf16[160,4096]{1,0:T(8,128)(2,1)S(1)}, bf16[160,4096]{1,0:T(8,128)(2,1)}, u32[]{:S(2)}) copy-start(bf16[160,4096]{1,0:T(8,128)(2,1)} %all-gather.8.cloned.1.call-done) | copy-start | bytes 3932164
Sparse Core Ops, SparseCore 0:
  9.6 20.8 all-gather.5
  34.2 32.6 all-gather.7
  80.2 51.0 reduce-scatter.2
  133.4 32.3 all-gather.9
  225.0 182.9 all-gather.11
  440.1 69.9 reduce-scatter.4
